TPU v7x, 256 devices: a whole 4x4x8 slice. The times are simulated.
256 devices in a mesh: dp: 64 (over x, z_lo, y), pipe: 4 (over z_hi, core).
Axes of the slice: x: 4, y: 4, z: 8 (z_hi: 2, z_lo: 4; z = z_hi * 4 + z_lo), core: 2. Of those that a mesh axis runs over, the one named last changes fastest.
Arguments:
- hidden: bfloat16 [16384, 2048], P('dp'), may hold values from -16 to 16
- gain: float32 [2048], replicated, may hold values from 0.25 to 1.75
- w_value: bfloat16 [4, 2048, 2048], P('pipe', 'dp'), may hold values from -0.125 to 0.125
- d_value: bfloat16 [4, 16384, 2048], P('pipe', 'dp'), may hold values from -3 to 3
Outputs:
- grad_hidden: bfloat16 [16384, 2048], P('dp')
- grad_gain: float32 [2048], P('dp')
- grad_value: float32 [4, 2048, 2048], P('pipe', 'dp')
All inputs are finite; a program needn't handle non-finite values.
Results may differ from a plain program's by a relative error of at most 0.0029.
Values may be sent and summed in bfloat16 or wider, within the bound.
No kernel may reach another device: no remote copies, remote signals or barrier semaphores. Data moves between devices by JAX's collectives and lax.ppermute only.
A program may use at most 64 MiB of HBM per device.

v0:
```python
import jax
import jax.numpy as jnp
from jax import lax
from jax.sharding import PartitionSpec as P

epsilon = 1e-06


def norm_backward(grad_rows, normed_rows, scale_rows, gain):
    scaled = gain * grad_rows
    result = (
        scaled - normed_rows * jnp.mean(scaled * normed_rows, axis=-1, keepdims=True)
    ) / scale_rows
    return (result.astype(jnp.bfloat16), jnp.sum(grad_rows * normed_rows, axis=0))


def weight_term(encoded, operand):
    return lax.dot_general(
        encoded, operand, (((0,), (0,)), ((), ())), preferred_element_type=jnp.float32
    )


def local(hidden, gain, w_value, d_value):
    hidden_f = hidden.astype(jnp.float32)
    row_scale = jnp.sqrt(jnp.mean(hidden_f * hidden_f, axis=-1, keepdims=True) + epsilon)
    normed = hidden_f / row_scale
    encoded = (normed * gain).astype(jnp.bfloat16)
    cotangent = d_value[0]
    projection = w_value[0]
    average = 1.0 / lax.axis_size("dp")
    partial_value = lax.dot_general(
        cotangent,
        lax.all_gather(projection, "dp", axis=0, tiled=True),
        (((1,), (1,)), ((), ())),
        preferred_element_type=jnp.float32,
    )
    grad_encoded = lax.psum(partial_value, "pipe")
    grad_hidden, gain_part = norm_backward(grad_encoded, normed, row_scale, gain)
    gain_share = lax.psum_scatter(gain_part, "dp", scatter_dimension=0, tiled=True)
    grad_gain = gain_share * average
    value_grad = (
        lax.psum_scatter(weight_term(encoded, cotangent), "dp", scatter_dimension=0, tiled=True)
        * average
    )
    return (grad_hidden, grad_gain, value_grad[None])


def solution(mesh):
    return jax.shard_map(
        local,
        mesh=mesh,
        in_specs=(P("dp", None), P(), P("pipe", "dp", None), P("pipe", "dp", None)),
        out_specs=(P("dp", None), P("dp"), P("pipe", "dp", None)),
        check_vma=False,
    )
```

profile of v0, /device:TPU:0, one launch (start us, length us, event | category | flops | bytes accessed | tf_op | source)
XLA Modules:
  0.0 898.9 jit_solution(13786770550400615789)
XLA Ops:
  7.2 0.0 copy-start
  7.2 0.0 all-gather.3.cloned.1.call-start
  7.2 0.7 all-gather.3.cloned.1.call-update
  7.9 0.0 all-reduce.3.cloned.1.call-start
  8.0 363.1 %all-gather.3.cloned.1.call-done = bf16[1,2048,2048]{2,1,0:T(8,128)(2,1)} async-done(((bf16[1,32,2048]{2,1,0:T(8,128)(2,1)}), bf16[1,2048,2048]{2,1,0:T(8,128)(2,1)}) %all-gather.3.cloned.1.call-update) | async-done | bytes 8388624 | tf_op jit(solution)/shard_map/all_gather | solution.py:33
  371.1 0.0 copy-done
  371.1 7.1 fusion
  378.2 0.0 copy-start.1
  378.2 0.0 copy-start.2
  378.2 0.0 all-reduce.3.cloned.1.call-update
  378.2 0.0 reduce-scatter.2.cloned.1.call-start
  378.3 1.1 copy-done.1
  379.4 0.3 fusion.2
  379.7 0.0 copy-done.2
  379.7 8.4 fusion.3
  388.1 0.0 copy-start.3
  388.1 0.0 reduce-scatter.2.cloned.1.call-update
  388.1 0.7 copy-done.3
  388.8 0.6 dynamic-slice
  390.0 87.9 %all-reduce.3.cloned.1.call-done = f32[256,2048]{1,0:T(8,128)} async-done(((f32[256,2048]{1,0:T(8,128)}), f32[256,2048]{1,0:T(8,128)}) %all-reduce.3.cloned.1.call-update) | async-done | bytes 2097168 | tf_op jit(solution)/shard_map/psum | solution.py:37
  478.0 2.2 multiply_reduce_fusion
  480.2 187.4 %all-reduce = f32[2048]{0:T(1024)S(1)} all-reduce(f32[2048]{0:T(1024)S(1)} %get-tuple-element.3), channel_id=3, replica_groups=mesh['dp'=64,'pipe'=4] {'dp'}, use_global_device_ids=true, to_apply=%region_4.0.clone | all-reduce | flops 2048 | bytes 16384
  667.6 0.6 dynamic-slice_multiply_fusion
  668.2 3.1 divide_convert_fusion
  671.3 219.4 %reduce-scatter.2.cloned.1.call-done = f32[32,2048]{1,0:T(8,128)} async-done(((f32[2048,2048]{1,0:T(8,128)}), f32[32,2048]{1,0:T(8,128)}) %reduce-scatter.2.cloned.1.call-update) | async-done | bytes 262160 | tf_op jit(solution)/shard_map/reduce_scatter | solution.py:42
  890.7 1.7 multiply_bitcast_fusion
  (2 shorter events, 0.0 us)
Async XLA Ops:
  7.2 363.9 %copy-start = (bf16[1,256,2048]{2,1,0:T(8,128)(2,1)S(1)}, bf16[1,256,2048]{2,1,0:T(8,128)(2,1)}, u32[]{:S(2)}) copy-start(bf16[1,256,2048]{2,1,0:T(8,128)(2,1)} %param.7) | copy-start | bytes 3145732
  7.2 363.9 %all-gather.3.cloned.1.call-start = ((), (), s32[]{:S(2)}) async-start(), calls=%async_computation.3 | async-start | bytes 8519680 | tf_op jit(solution)/shard_map/all_gather | solution.py:33
  7.9 470.0 %all-reduce.3.cloned.1.call-start = ((), (), s32[]{:S(2)}) async-start(), calls=%async_computation.1 | async-start | bytes 4194304 | tf_op jit(solution)/shard_map/psum | solution.py:37
  378.2 1.2 copy-start.1
  378.2 1.5 copy-start.2
  378.2 512.4 %reduce-scatter.2.cloned.1.call-start = ((), (), s32[]{:S(2)}) async-start(), calls=%async_computation.2 | async-start | bytes 17039360 | tf_op jit(solution)/shard_map/reduce_scatter | solution.py:42
  388.1 0.7 copy-start.3
Sparse Core Ops, SparseCore 0:
  9.8 361.2 all-gather.2
  378.3 99.5 all-reduce.2
  480.5 410.0 reduce-scatter.1
where the time goes:
time: 899 us
  waiting for transfers between devices  671 us (75%)
  blocking collectives  187 us (21%)
  matrix products  15.5 us (2%)
  between operations  14.4 us (2%)
    all_gather x1, waiting for transfers between devices, local(): lax.all_gather(projection, 'dp', axis=0, tiled=True)  363 us
    reduce_scatter x1, waiting for transfers between devices, local(): lax.psum_scatter(weight_term(encoded, cotangent), 'dp', scatter_dimension...  219 us
    unnamed x1, blocking collectives  187 us
    psum x1, waiting for transfers between devices, local(): grad_encoded = lax.psum(partial_value, 'pipe')  87.9 us
  transfers between devices with their start and end apart: 3, of which 3 were waited for; matrix products, arithmetic and copies ran while one was open for 2% of the time, Pallas kernels for 0%

commit v1 on v0

--- a/solution.py
+++ b/solution.py
@@ -30,7 +30,9 @@
     average = 1.0 / lax.axis_size("dp")
     partial_value = lax.dot_general(
         cotangent,
-        lax.all_gather(projection, "dp", axis=0, tiled=True),
+        jnp.concatenate(
+            lax.all_to_all(jnp.stack([projection] * lax.axis_size("dp")), "dp", 0, 0), axis=0
+        ),
         (((1,), (1,)), ((), ())),
         preferred_element_type=jnp.float32,
     )

time: 899 us -> 679 us (0.76)
  waiting for transfers between devices: 671 us -> 249 us
  blocking collectives: 187 us -> 383 us
    all_gather x1 -> x0, waiting for transfers between devices: 363 us -> none  [local(): lax.all_gather(projection, 'dp', axis=0, tiled=True)]
    all_to_all x0 -> x1, blocking collectives: none -> 197 us  [local(): lax.all_to_all(jnp.stack([projection] * lax.axis_size('dp')), 'dp', 0, 0)]
    reduce_scatter x1, waiting for transfers between devices: 219 us -> 161 us  [local(): lax.psum_scatter(weight_term(encoded, cotangent), 'dp', scatter_dimension...]
  transfers between devices with their start and end apart: 3 -> 2, of which waited for: 3 -> 2; matrix products, arithmetic and copies ran while one was open for 2% -> 2% of each run, Pallas kernels for 0% -> 0%
where the time goes in v1:
time: 679 us; the launch traced here: 673 us
  blocking collectives  383 us (56%)
  waiting for transfers between devices  249 us (37%)
  between operations  16.2 us (2%)
  matrix products  12.1 us (2%)
  other arithmetic  7.9 us (1%)
    all_to_all x1, blocking collectives, local(): lax.all_to_all(jnp.stack([projection] * lax.axis_size('dp')), 'dp', 0, 0)  197 us
    unnamed x1, blocking collectives  186 us
    reduce_scatter x1, waiting for transfers between devices, local(): lax.psum_scatter(weight_term(encoded, cotangent), 'dp', scatter_dimension...  161 us
    psum x1, waiting for transfers between devices, local(): grad_encoded = lax.psum(partial_value, 'pipe')  88.5 us
  transfers between devices with their start and end apart: 2, of which 2 were waited for; matrix products, arithmetic and copies ran while one was open for 2% of the time, Pallas kernels for 0%

profile of v1, /device:TPU:0, one launch (start us, length us, event | category | flops | bytes accessed | tf_op | source)
XLA Modules:
  0.0 673.3 jit_solution(12812859549229055097)
XLA Ops:
  8.0 0.0 copy-start
  8.0 0.0 all-reduce.3.cloned.1.call-start
  8.1 2.0 stack.3
  10.1 197.0 %all_to_all.5 = bf16[64,32,2048]{2,1,0:T(8,128)(2,1)S(1)} all-to-all(bf16[64,32,2048]{2,1,0:T(8,128)(2,1)S(1)} %stack.3), channel_id=1, replica_groups=mesh['dp'=64,'pipe'=4] {'dp'}, dimensions={0} | all-to-all | bytes 16777216 | tf_op jit(solution)/shard_map/all_to_all | solution.py:34
  207.0 0.0 copy-done
  207.1 3.7 fusion.3
  210.7 0.0 copy-start.1
  210.7 0.0 copy-start.2
  210.7 0.0 all-reduce.3.cloned.1.call-update
  210.7 0.0 reduce-scatter.2.cloned.1.call-start
  210.8 1.1 copy-done.1
  211.9 0.3 fusion
  212.2 0.0 copy-done.2
  212.2 8.4 %fusion.1 = f32[2048,2048]{1,0:T(8,128)} fusion(bf16[1,256,2048]{2,1,0:T(8,128)(2,1)S(1)} %copy-done, f32[2048]{0:T(1024)S(1)} %copy-done.2, bf16[256,2048]{1,0:T(8,128)(2,1)S(1)} %copy-done.1, f32[256]{0:T(256)S(1)} %add_sqrt_fusion), kind=kOutput, calls=%fused_computation.7 | convolution fusion | flops 2149580800 | bytes 18883584 | tf_op jit(solution)/shard_map/dot_general | solution.py:18
  220.7 0.0 copy-start.3
  220.7 0.0 reduce-scatter.2.cloned.1.call-update
  220.7 0.6 copy-done.3
  221.3 0.6 dynamic-slice
  222.6 88.5 %all-reduce.3.cloned.1.call-done = f32[256,2048]{1,0:T(8,128)} async-done(((f32[256,2048]{1,0:T(8,128)}), f32[256,2048]{1,0:T(8,128)}) %all-reduce.3.cloned.1.call-update) | async-done | bytes 2097168 | tf_op jit(solution)/shard_map/psum | solution.py:39
  311.1 2.3 multiply_reduce_fusion
  313.3 186.4 %all-reduce = f32[2048]{0:T(1024)S(1)} all-reduce(f32[2048]{0:T(1024)S(1)} %get-tuple-element.3), channel_id=2, replica_groups=mesh['dp'=64,'pipe'=4] {'dp'}, use_global_device_ids=true, to_apply=%region_4.0.clone | all-reduce | flops 2048 | bytes 16384
  499.7 0.6 dynamic-slice_multiply_fusion
  500.3 3.1 divide_convert_fusion
  503.4 160.8 %reduce-scatter.2.cloned.1.call-done = f32[32,2048]{1,0:T(8,128)} async-done(((f32[2048,2048]{1,0:T(8,128)}), f32[32,2048]{1,0:T(8,128)}) %reduce-scatter.2.cloned.1.call-update) | async-done | bytes 262160 | tf_op jit(solution)/shard_map/reduce_scatter | solution.py:44
  664.2 1.7 multiply_bitcast_fusion
  (2 shorter events, 0.0 us)
Async XLA Ops:
  8.0 199.1 %copy-start = (bf16[1,256,2048]{2,1,0:T(8,128)(2,1)S(1)}, bf16[1,256,2048]{2,1,0:T(8,128)(2,1)}, u32[]{:S(2)}) copy-start(bf16[1,256,2048]{2,1,0:T(8,128)(2,1)} %param.7) | copy-start | bytes 3145732
  8.0 303.0 %all-reduce.3.cloned.1.call-start = ((), (), s32[]{:S(2)}) async-start(), calls=%async_computation.2 | async-start | bytes 4194304 | tf_op jit(solution)/shard_map/psum | solution.py:39
  210.7 1.2 copy-start.1
  210.7 1.5 copy-start.2
  210.7 453.5 %reduce-scatter.2.cloned.1.call-start = ((), (), s32[]{:S(2)}) async-start(), calls=%async_computation.3 | async-start | bytes 17039360 | tf_op jit(solution)/shard_map/reduce_scatter | solution.py:44
  220.7 0.7 copy-start.3
Sparse Core Ops, SparseCore 0:
  210.9 100.1 all-reduce.2
Sparse Core Ops, SparseCore 1:
  220.8 443.4 reduce-scatter.1
